TPU v7x, 256 devices: a whole 4x4x8 slice. The times are simulated.
256 devices in a mesh: walk: 64 (over z, x, core), elec: 2 (over y_lo), chol: 2 (over y_hi).
Axes of the slice: x: 4, y: 4 (y_hi: 2, y_lo: 2; y = y_hi * 2 + y_lo), z: 8, core: 2. Of those that a mesh axis runs over, the one named last changes fastest.
Arguments:
- green: bfloat16 [64, 1024, 256], P('walk'), may hold values from -6 to 6
- chol_vecs: bfloat16 [128, 256, 1024], P(('walk', 'chol'), 'elec'), may hold values from -0.1875 to 0.1875
Outputs:
- gradient: float32 [64, 1024, 256], P('walk', ('elec', 'chol'))
All inputs are finite; a program needn't handle non-finite values.
Results may differ from a plain program's by a relative error of at most 0.0029.
Values may be sent and summed in bfloat16 or wider, within the bound.
No kernel may reach another device: no remote copies, remote signals or barrier semaphores. Data moves between devices by JAX's collectives and lax.ppermute only.
A program may use at most 64 MiB of HBM per device.

v0:
```python
import jax
import jax.numpy as jnp
from jax import lax
from jax.sharding import PartitionSpec as P


def cut_along(value, dim, devices):
    dims = value.shape
    pieces = value.reshape(*dims[:dim], devices, dims[dim] // devices, *dims[dim + 1 :])
    return jnp.moveaxis(pieces, dim, 0)


def sent_and_summed(value, axis, dim):
    devices = lax.axis_size(axis)
    pieces = lax.all_to_all(cut_along(value, dim, devices), axis, 0, 0, tiled=True)
    return jnp.sum(pieces, axis=0)


def shards(green, chol_vecs):
    walkers, orbitals, electrons = green.shape
    starting = jnp.zeros((walkers, orbitals, electrons), jnp.float32)
    blocks = lax.all_gather(chol_vecs, "walk", axis=0, tiled=True)
    number = blocks.shape[0]
    own_rows = blocks.shape[1]
    intersection = jnp.einsum(
        "gap,wpb->gwab", blocks, green, preferred_element_type=jnp.float32
    ).astype(jnp.bfloat16)
    flattened = intersection.reshape(number * walkers, own_rows, electrons)
    received = lax.all_to_all(flattened, "elec", split_axis=2, concat_axis=1, tiled=True)
    received = received.reshape(number, walkers, electrons, own_rows)
    running = starting - jnp.einsum(
        "gap,gwba->wpb", blocks, received, preferred_element_type=jnp.float32
    )
    return sent_and_summed(running, ("elec", "chol"), 1)


def solution(mesh):
    in_specs = (P("walk", None, None), P(("walk", "chol"), "elec", None))
    out_specs = P("walk", ("elec", "chol"), None)
    return jax.shard_map(shards, mesh=mesh, in_specs=in_specs, out_specs=out_specs, check_vma=False)
```

profile of v0, /device:TPU:1, one launch (start us, length us, event | category | flops | bytes accessed | tf_op | source)
XLA Modules:
  0.0 216.9 jit_solution(13085413836040828530)
XLA Ops:
  6.5 0.0 copy-start
  6.5 0.0 all-gather.2.cloned.1.call-start
  6.5 0.7 all-gather.2.cloned.1.call-update
  7.3 106.3 %all-gather.2.cloned.1.call-done = bf16[64,128,1024]{2,1,0:T(8,128)(2,1)} async-done(((bf16[1,128,1024]{2,1,0:T(8,128)(2,1)}), bf16[64,128,1024]{2,1,0:T(8,128)(2,1)}) %all-gather.2.cloned.1.call-update) | async-done | bytes 16777232 | tf_op jit(solution)/shard_map/all_gather | solution.py:22
  113.5 0.0 copy-done
  113.5 8.2 %convert_bitcast_fusion = bf16[64,128,256]{1,2,0:T(8,128)(2,1)S(1)} fusion(bf16[64,128,1024]{2,1,0:T(8,128)(2,1)} %all-gather.2.cloned.1.call-done, bf16[1,1024,256]{2,1,0:T(8,128)(2,1)S(1)} %copy-done), kind=kOutput, calls=%fused_computation | convolution fusion | flops 4297064448 | bytes 21495808 | tf_op jit(solution)/shard_map/gap,wpb->gwab/dot_general | solution.py:25
  121.8 2.7 %copy.6 = bf16[64,128,256]{1,0,2:T(8,128)(2,1)S(1)} copy(bf16[64,128,256]{1,2,0:T(8,128)(2,1)S(1)} %convert_bitcast_fusion) | data formatting | bytes 8388608 | tf_op jit(solution)/shard_map/reshape | solution.py:28
  124.5 50.9 %all_to_all.20 = bf16[64,128,256]{1,0,2:T(8,128)(2,1)} all-to-all(bf16[64,128,256]{1,0,2:T(8,128)(2,1)S(1)} %copy.6), channel_id=1, replica_groups=mesh['walk'=64,'elec'=2,'chol'=2] {'elec'}, dimensions={2} | all-to-all | bytes 8388608 | tf_op jit(solution)/shard_map/all_to_all | solution.py:29
  175.3 6.9 %copy.7 = bf16[64,128,2,128]{3,1,2,0:T(8,128)(2,1)} copy(bf16[64,128,2,128]{1,0,3,2:T(8,128)(2,1)} %bitcast.30) | data formatting | bytes 8388608 | tf_op jit(solution)/shard_map/all_to_all | solution.py:29
  182.2 9.7 %fusion = f32[256,1024]{1,0:T(8,128)S(1)} fusion(bf16[64,256,128]{2,1,0:T(8,128)(2,1)} %bitcast.31, bf16[64,128,1024]{2,1,0:T(8,128)(2,1)} %all-gather.2.cloned.1.call-done), kind=kOutput, calls=%fused_computation.2 | convolution fusion | flops 4295229440 | bytes 22020096 | tf_op jit(solution)/shard_map/gap,gwba->wpb/dot_general | solution.py:31
  192.0 0.1 copy.16
  192.1 17.1 %all_to_all.21 = f32[4,1,256,256]{2,3,1,0:T(8,128)S(1)} all-to-all(f32[4,1,256,256]{2,3,1,0:T(8,128)S(1)} %bitcast.32), channel_id=1, replica_groups=mesh['walk'=64,'elec'=2,'chol'=2] {'elec','chol'}, dimensions={0} | all-to-all | bytes 2097152 | tf_op jit(solution)/shard_map/all_to_all | solution.py:15
  209.2 0.1 reduce_sum.11
  209.3 0.8 copy.10
Async XLA Ops:
  6.5 107.0 %copy-start = (bf16[1,1024,256]{2,1,0:T(8,128)(2,1)S(1)}, bf16[1,1024,256]{2,1,0:T(8,128)(2,1)}, u32[]{:S(2)}) copy-start(bf16[1,1024,256]{2,1,0:T(8,128)(2,1)} %param.2) | copy-start | bytes 1572868
  6.5 107.0 %all-gather.2.cloned.1.call-start = ((), (), s32[]{:S(2)}) async-start(), calls=%async_computation.2 | async-start | bytes 17039360 | tf_op jit(solution)/shard_map/all_gather | solution.py:22
Sparse Core Ops, SparseCore 0:
  10.1 103.3 all-gather.1
where the time goes:
time: 217 us
  waiting for transfers between devices  107 us (49%)
  blocking collectives  68 us (31%)
  matrix products  17.9 us (8%)
  between operations  13.4 us (6%)
  local copies, waits for them, and re-layouts  10.5 us (5%)
    all_gather x1, waiting for transfers between devices, shards(): blocks = lax.all_gather(chol_vecs, 'walk', axis=0, tiled=True)  106 us
    all_to_all x1, blocking collectives, shards(): lax.all_to_all(flattened, 'elec', split_axis=2, concat_axis=1, tiled=True)  50.9 us
    all_to_all x1, blocking collectives, sent_and_summed(): lax.all_to_all(cut_along(value, dim, devices), axis, 0, 0, tiled=True)  17.1 us
    dot_general x1, matrix products, shards(): jnp.einsum('gap,gwba->wpb', blocks, received, preferred_element_type=jnp....  9.74 us
    dot_general x1, matrix products, shards(): jnp.einsum('gap,wpb->gwab', blocks, green, preferred_element_type=jnp.flo...  8.21 us
    all_to_all x1, local copies, waits for them, and re-layouts, shards(): lax.all_to_all(flattened, 'elec', split_axis=2, concat_axis=1, tiled=True)  6.87 us
  transfers between devices with their start and end apart: 1, of which 1 were waited for; matrix products, arithmetic and copies ran while one was open for 0% of the time, Pallas kernels for 0%

commit v1 on v0

--- a/solution.py
+++ b/solution.py
@@ -2,6 +2,7 @@
 import jax.numpy as jnp
 from jax import lax
 from jax.sharding import PartitionSpec as P
+from jax.lax import all_to_all, axis_size
 
 
 def cut_along(value, dim, devices):
@@ -19,7 +20,16 @@
 def shards(green, chol_vecs):
     walkers, orbitals, electrons = green.shape
     starting = jnp.zeros((walkers, orbitals, electrons), jnp.float32)
-    blocks = lax.all_gather(chol_vecs, "walk", axis=0, tiled=True)
+    cut_points = lambda frame_in: jnp.concatenate(
+        all_to_all(
+            jnp.stack([frame_in for _ in range(axis_size("walk"))]),
+            "walk",
+            split_axis=0,
+            concat_axis=0,
+        ),
+        axis=0,
+    )
+    blocks = cut_points(chol_vecs)
     number = blocks.shape[0]
     own_rows = blocks.shape[1]
     intersection = jnp.einsum(

time: 217 us -> 479 us (2.21); the launches traced: 217 us -> 474 us
  blocking collectives: 68 us -> 442 us
  waiting for transfers between devices: 107 us -> 0 us
  between operations: 13.4 us -> 0.05 us
    all_to_all x0 -> x1, blocking collectives: none -> 377 us  [shards(): all_to_all(jnp.stack([frame_in for _ in range(axis_size('walk'))]), 'walk...]
    all_gather x1 -> x0, waiting for transfers between devices: 106 us -> none  [shards(): blocks = lax.all_gather(chol_vecs, 'walk', axis=0, tiled=True)]
  transfers between devices with their start and end apart: 1 -> 0, of which waited for: 1 -> 0; matrix products, arithmetic and copies ran while one was open for 0% -> 0% of each run, Pallas kernels for 0% -> 0%
where the time goes in v1:
time: 479 us; the launch traced here: 474 us
  blocking collectives  442 us (92%)
  matrix products  17.9 us (4%)
  local copies, waits for them, and re-layouts  13.9 us (3%)
    all_to_all x1, blocking collectives, shards(): all_to_all(jnp.stack([frame_in for _ in range(axis_size('walk'))]), 'walk...  377 us
    all_to_all x1, blocking collectives, shards(): lax.all_to_all(flattened, 'elec', split_axis=2, concat_axis=1, tiled=True)  49.1 us
    all_to_all x1, blocking collectives, sent_and_summed(): lax.all_to_all(cut_along(value, dim, devices), axis, 0, 0, tiled=True)  15.7 us
    dot_general x1, matrix products, shards(): jnp.einsum('gap,gwba->wpb', blocks, received, preferred_element_type=jnp....  9.74 us

profile of v1, /device:TPU:1, one launch (start us, length us, event | category | flops | bytes accessed | tf_op | source)
XLA Modules:
  0.0 473.9 jit_solution(12670595391196287009)
XLA Ops:
  0.0 0.0 copy-start
  0.0 3.4 stack.2
  3.4 377.2 %all_to_all.25 = bf16[64,1,128,1024]{3,2,1,0:T(8,128)(2,1)} all-to-all(bf16[64,1,128,1024]{3,2,1,0:T(8,128)(2,1)S(1)} %stack.2), channel_id=1, replica_groups=mesh['walk'=64,'elec'=2,'chol'=2] {'walk'}, dimensions={0} | all-to-all | bytes 33554432 | tf_op jit(solution)/shard_map/all_to_all | solution.py:24
  380.6 0.0 copy-done
  380.6 8.2 %convert_bitcast_fusion = bf16[64,128,256]{1,2,0:T(8,128)(2,1)S(1)} fusion(bf16[64,1,128,1024]{3,2,1,0:T(8,128)(2,1)} %all_to_all.25, bf16[1,1024,256]{2,1,0:T(8,128)(2,1)S(1)} %copy-done), kind=kOutput, calls=%fused_computation.4 | convolution fusion | flops 4297064448 | bytes 21495808 | tf_op jit(solution)/shard_map/gap,wpb->gwab/dot_general | solution.py:35
  388.8 2.7 copy.6
  391.5 49.1 %all_to_all.26 = bf16[64,128,256]{1,0,2:T(8,128)(2,1)} all-to-all(bf16[64,128,256]{1,0,2:T(8,128)(2,1)S(1)} %copy.6), channel_id=1, replica_groups=mesh['walk'=64,'elec'=2,'chol'=2] {'elec'}, dimensions={2} | all-to-all | bytes 8388608 | tf_op jit(solution)/shard_map/all_to_all | solution.py:39
  440.6 6.9 %copy.7 = bf16[64,128,2,128]{3,1,2,0:T(8,128)(2,1)} copy(bf16[64,128,2,128]{1,0,3,2:T(8,128)(2,1)} %bitcast.40) | data formatting | bytes 8388608 | tf_op jit(solution)/shard_map/all_to_all | solution.py:39
  447.5 9.7 %fusion.9 = f32[256,1024]{1,0:T(8,128)S(1)} fusion(bf16[64,256,128]{2,1,0:T(8,128)(2,1)} %bitcast.41, bf16[64,1,128,1024]{3,2,1,0:T(8,128)(2,1)} %all_to_all.25), kind=kOutput, calls=%fused_computation.6 | convolution fusion | flops 4295229440 | bytes 22020096 | tf_op jit(solution)/shard_map/gap,gwba->wpb/dot_general | solution.py:41
  457.2 0.1 copy.16
  457.3 15.7 %all_to_all.27 = f32[4,1,256,256]{2,3,1,0:T(8,128)S(1)} all-to-all(f32[4,1,256,256]{2,3,1,0:T(8,128)S(1)} %bitcast.42), channel_id=1, replica_groups=mesh['walk'=64,'elec'=2,'chol'=2] {'elec','chol'}, dimensions={0} | all-to-all | bytes 2097152 | tf_op jit(solution)/shard_map/all_to_all | solution.py:16
  473.0 0.1 reduce_sum.11
  473.1 0.8 copy.10
Async XLA Ops:
  0.0 380.6 %copy-start = (bf16[1,1024,256]{2,1,0:T(8,128)(2,1)S(1)}, bf16[1,1024,256]{2,1,0:T(8,128)(2,1)}, u32[]{:S(2)}) copy-start(bf16[1,1024,256]{2,1,0:T(8,128)(2,1)} %param.2) | copy-start | bytes 1572868
